TPU v7x, 32 devices: a whole 2x2x4 slice. The times are simulated.
32 devices in a mesh: member: 2 (over y), lon: 4 (over z), lat: 2 (over x), dp: 2 (over core).
Axes of the slice: x: 2, y: 2, z: 4, core: 2. Of those that a mesh axis runs over, the one named last changes fastest.
Arguments:
- fields: bfloat16 [4, 64, 32, 512], P(('member', 'dp'), 'lat', 'lon'), parts along dimension 0, may hold values from -6 to 6
- cotangent: bfloat16 [4, 64, 32, 512], P(('member', 'dp'), 'lat', 'lon'), parts along dimension 0, may hold values from -6 to 6
- conv_weight: float32 [7, 7, 512], replicated, may hold values from -0.875 to 0.875
- norm_gain: float32 [512], replicated, may hold values from 0.1 to 1.9
- w_qkv: bfloat16 [512, 768], replicated, may hold values from -1 to 1
- w_out: bfloat16 [256, 512], replicated, may hold values from -0.375 to 0.375
Outputs:
- result: bfloat16 [4, 64, 32, 512], P(('member', 'dp'), 'lat', 'lon'), parts along dimension 0
- grad_fields: bfloat16 [4, 64, 32, 512], P(('member', 'dp'), 'lat', 'lon'), parts along dimension 0
- grad_qkv: float32 [1024, 768], P('member'), parts along dimension 0
- grad_out: float32 [512, 512], P('member'), parts along dimension 0
- grad_conv: float32 [14, 7, 512], P('member'), parts along dimension 0
- grad_gain: float32 [1024], P('member'), parts along dimension 0
There are 2 independent parts, one for each index of `member`. A program takes and returns all parts, laid end to end along the dimension named above; an argument that names none is the same for every part. Nothing has to cross between parts.
All inputs are finite; a program needn't handle non-finite values.
Results may differ from a plain program's by a relative error of at most 0.012.
The roundings to bfloat16 on the way count: a program that leaves them out, or rounds other values in their place, can miss the bound.
Values may be sent and summed in bfloat16 or wider, within the bound.
A program may use at most 64 MiB of HBM per device.

v0:
```python
import jax
import jax.numpy as jnp
from jax import lax
from jax.sharding import PartitionSpec as P

HEADS = 4
HEAD_DIM = 64
EPSILON = 1e-06


def with_halo(x, sides, width, wrap):
    for axis, dim in sides:
        size, length = (lax.axis_size(axis), x.shape[dim])
        up = [(i, (i + 1) % size) for i in range(size if wrap else size - 1)]
        down = [(j, i) for i, j in up]
        last = lax.slice_in_dim(x, length - width, length, axis=dim)
        first = lax.slice_in_dim(x, 0, width, axis=dim)
        before = lax.ppermute(last, axis, up)
        after = lax.ppermute(first, axis, down)
        x = jnp.concatenate([before, x, after], axis=dim)
    return x


def spread(padded, kernel, lat_rows, lon_cols):
    summed = jnp.zeros(padded.shape[:1] + (lat_rows, lon_cols, padded.shape[3]), jnp.float32)
    for row_shift in range(7):
        band = padded[:, row_shift : row_shift + lat_rows].astype(jnp.float32)
        partial_row = kernel[row_shift, 0] * band[:, :, 0:lon_cols]
        for col_shift in range(1, 7):
            partial_row = (
                partial_row
                + kernel[row_shift, col_shift] * band[:, :, col_shift : col_shift + lon_cols]
            )
        summed = summed + partial_row
    return summed


def correlate(padded, upstream, lat_rows, lon_cols):
    pieces = []
    for row_shift in range(7):
        for col_shift in range(7):
            window = padded[
                :, row_shift : row_shift + lat_rows, col_shift : col_shift + lon_cols
            ].astype(jnp.float32)
            pieces.append(jnp.sum(window * upstream, axis=(0, 1, 2)))
    return jnp.stack(pieces).reshape(7, 7, -1)


def split_heads(values):
    return values.reshape(values.shape[:-1] + (HEADS, HEAD_DIM))


def attend_forward(rowwise, att_width):
    queries = split_heads(rowwise[..., :att_width])
    keys_part = split_heads(rowwise[..., att_width : 2 * att_width])
    values_part = split_heads(rowwise[..., 2 * att_width :])
    scores = jnp.einsum(
        "brqhd,brkhd->brhqk", queries, keys_part, preferred_element_type=jnp.float32
    ) * HEAD_DIM ** (-0.5)
    row_peak = jnp.max(scores, -1, keepdims=True)
    raised = jnp.exp(scores - row_peak)
    probs = raised / jnp.sum(raised, -1, keepdims=True)
    weights = probs.astype(jnp.bfloat16)
    mixed = jnp.einsum(
        "brhqk,brkhd->brqhd", weights, values_part, preferred_element_type=jnp.float32
    )
    return (mixed.reshape(rowwise.shape[:3] + (att_width,)).astype(jnp.bfloat16), probs)


def attend_backward(rowwise, probs, grad_rowwise, att_width):
    queries = split_heads(rowwise[..., :att_width])
    keys_part = split_heads(rowwise[..., att_width : 2 * att_width])
    values_part = split_heads(rowwise[..., 2 * att_width :])
    grad_heads = split_heads(grad_rowwise)
    weights = probs.astype(jnp.bfloat16)
    grad_probs = jnp.einsum(
        "brqhd,brkhd->brhqk", grad_heads, values_part, preferred_element_type=jnp.float32
    )
    inner = jnp.sum(probs * grad_probs, -1, keepdims=True)
    grad_scores = (probs * (grad_probs - inner) * HEAD_DIM ** (-0.5)).astype(jnp.bfloat16)
    grad_query = jnp.einsum(
        "brhqk,brkhd->brqhd", grad_scores, keys_part, preferred_element_type=jnp.float32
    )
    grad_key = jnp.einsum(
        "brhqk,brqhd->brkhd", grad_scores, queries, preferred_element_type=jnp.float32
    )
    grad_value = jnp.einsum(
        "brhqk,brqhd->brkhd", weights, grad_heads, preferred_element_type=jnp.float32
    )
    shaped = rowwise.shape[:3] + (att_width,)
    return jnp.concatenate(
        [
            grad_query.reshape(shaped).astype(jnp.bfloat16),
            grad_key.reshape(shaped).astype(jnp.bfloat16),
            grad_value.reshape(shaped).astype(jnp.bfloat16),
        ],
        axis=-1,
    )


def contract_rows(left, right):
    return lax.dot_general(
        left, right, (((0,), (0,)), ((), ())), preferred_element_type=jnp.float32
    )


def contract_cols(left, right):
    return lax.dot_general(
        left, right, (((1,), (1,)), ((), ())), preferred_element_type=jnp.float32
    )


def on_device(fields, cotangent, conv_weight, norm_gain, w_qkv, w_out):
    batch_count, lat_rows, lon_cols, channels = fields.shape
    att_width = w_out.shape[0]
    wide = with_halo(fields, (("lon", 2),), 3, True)
    padded = with_halo(wide, (("lat", 1),), 3, False)
    update = fields.astype(jnp.float32) + spread(padded, conv_weight, lat_rows, lon_cols)
    inverse = lax.rsqrt(jnp.mean(update * update, -1, keepdims=True) + EPSILON)
    normed = (update * inverse * norm_gain).astype(jnp.bfloat16)
    normed_flat = normed.reshape(-1, channels)
    projected = jnp.dot(normed_flat, w_qkv, preferred_element_type=jnp.float32).astype(jnp.bfloat16)
    rowwise = lax.all_to_all(
        projected.reshape(batch_count, lat_rows, lon_cols, 3 * att_width),
        "lon",
        split_axis=1,
        concat_axis=2,
        tiled=True,
    )
    mixed_rows, probs = attend_forward(rowwise, att_width)
    mixed = lax.all_to_all(mixed_rows, "lon", split_axis=2, concat_axis=1, tiled=True)
    mixed_flat = mixed.reshape(-1, att_width)
    result = (
        update
        + jnp.dot(mixed_flat, w_out, preferred_element_type=jnp.float32).reshape(update.shape)
    ).astype(jnp.bfloat16)
    upstream_flat = cotangent.reshape(-1, channels)
    grad_mixed = contract_cols(upstream_flat, w_out).astype(jnp.bfloat16)
    grad_out = contract_rows(mixed_flat, upstream_flat)
    grad_rowwise = lax.all_to_all(
        grad_mixed.reshape(batch_count, lat_rows, lon_cols, att_width),
        "lon",
        split_axis=1,
        concat_axis=2,
        tiled=True,
    )
    grad_projected_rows = attend_backward(rowwise, probs, grad_rowwise, att_width)
    grad_projected = lax.all_to_all(
        grad_projected_rows, "lon", split_axis=2, concat_axis=1, tiled=True
    )
    grad_flat = grad_projected.reshape(-1, 3 * att_width)
    grad_weight = contract_rows(normed_flat, grad_flat)
    grad_normed = contract_cols(grad_flat, w_qkv).reshape(update.shape)
    grad_gain = jnp.sum(grad_normed * (update * inverse), axis=(0, 1, 2))
    gained = norm_gain * grad_normed
    grad_update = (
        cotangent.astype(jnp.float32)
        + inverse * gained
        - update * inverse**3 * jnp.mean(gained * update, -1, keepdims=True)
    )
    grad_wide = with_halo(grad_update.astype(jnp.bfloat16), (("lon", 2),), 3, True).astype(
        grad_update.dtype
    )
    grad_padded = with_halo(grad_wide.astype(jnp.bfloat16), (("lat", 1),), 3, False).astype(
        grad_wide.dtype
    )
    grad_fields = (
        grad_update + spread(grad_padded, conv_weight[::-1, ::-1], lat_rows, lon_cols)
    ).astype(jnp.bfloat16)
    grad_conv = correlate(padded, grad_update, lat_rows, lon_cols)
    totals = lax.psum((grad_weight, grad_out, grad_conv, grad_gain), ("lon", "lat", "dp"))
    return (result, grad_fields, totals[0], totals[1], totals[2], totals[3])


def solution(mesh):
    placed = (
        P(("member", "dp"), "lat", "lon", None),
        P(("member", "dp"), "lat", "lon", None),
        P(),
        P(),
        P(),
        P(),
    )
    return jax.shard_map(
        on_device,
        mesh=mesh,
        in_specs=placed,
        out_specs=(
            P(("member", "dp"), "lat", "lon", None),
            P(("member", "dp"), "lat", "lon", None),
            P("member", None),
            P("member", None),
            P("member", None, None),
            P("member"),
        ),
        check_vma=False,
    )
```

profile of v0, /device:TPU:0, one launch (start us, length us, event | category | flops | bytes accessed | tf_op | source)
XLA Modules:
  0.0 233.1 jit_solution(6971295654083758024)
XLA Ops:
  7.2 1.2 fusion.160
  8.4 3.1 %collective-permute-start = (bf16[1,32,3,512]{3,2,1,0:T(4,128)(2,1)S(1)}, bf16[1,32,3,512]{3,2,1,0:T(4,128)(2,1)S(1)}, u32[]{:S(2)}, u32[]{:S(2)}) collective-permute-start(bf16[1,32,3,512]{3,2,1,0:T(4,128)(2,1)S(1)} %get-tuple-element.93), channel_id=1, source_target_pairs={{0,4},{4,8},{8,12},{12,0},{1,5},{5,9},{9,13},{13,1},{2,6},{6,10},{... | collective-permute-start | bytes 294920 | tf_op jit(solution)/shard_map/ppermute | solution.py:18
  11.6 2.1 collective-permute-start.1
  13.6 1.9 fusion.15
  15.6 3.9 %all-to-all-start.2 = ((bf16[1,32,8,256]{3,2,0,1:T(8,128)(2,1)}), bf16[1,32,8,256]{3,2,0,1:T(8,128)(2,1)}, u32[]{:S(2)}, u32[]{:S(2)}) async-start(bf16[1,32,8,256]{3,2,0,1:T(8,128)(2,1)} %fusion.15), calls=%async_computation.2 | async-start | bytes 262144 | tf_op jit(solution)/shard_map/all_to_all | solution.py:140
  19.6 0.6 fusion.161
  20.2 0.7 fusion.162
  20.9 1.2 fusion.156
  22.1 3.5 %collective-permute-start.2 = (bf16[1,3,14,512]{3,2,1,0:T(8,128)(2,1)S(1)}, bf16[1,3,14,512]{3,2,1,0:T(8,128)(2,1)S(1)}, u32[]{:S(2)}, u32[]{:S(2)}) collective-permute-start(bf16[1,3,14,512]{3,2,1,0:T(8,128)(2,1)S(1)} %get-tuple-element.84), channel_id=1, source_target_pairs={{0,2},{1,3},{4,6},{5,7},{8,10},{9,11},{12,14},{13,15},{16,18},{17,... | collective-permute-start | bytes 129032 | tf_op jit(solution)/shard_map/ppermute | solution.py:18
  25.7 1.3 collective-permute-start.3
  27.0 0.6 fusion.163
  27.6 4.0 %collective-permute-done.3 = bf16[1,3,14,512]{3,2,1,0:T(8,128)(2,1)S(1)} collective-permute-done((bf16[1,3,14,512]{3,2,1,0:T(8,128)(2,1)S(1)}, bf16[1,3,14,512]{3,2,1,0:T(8,128)(2,1)S(1)}, u32[]{:S(2)}, u32[]{:S(2)}) %collective-permute-start.3) | collective-permute-done | bytes 43040 | tf_op jit(solution)/shard_map/ppermute | solution.py:19
  31.7 0.3 maximum_maximum_fusion
  32.0 2.0 slice_convert_fusion.2
  34.0 10.5 %multiply_reduce_fusion.51 = (f32[32,8]{1,0:T(8,128)S(1)}, f32[1,32,8,512]{3,2,1,0:T(8,128)S(1)}) fusion(f32[1,32,14,512]{3,2,1,0:T(8,128)S(1)} %get-tuple-element.77, f32[512]{0:T(512)} %bitcast.283, f32[512]{0:T(512)} %bitcast.285, f32[512]{0:T(512)S(1)} %bitcast.191, f32[512]{0:T(512)S(1)} %bitcast.193, f32[512]{0:T(512)S(1)} %bitcast.195, ...), kind=kLoop, calls=%fused_computation.293 | loop fusion | flops 13238016 | bytes 26577920 | tf_op jit(solution)/shard_map/reduce_sum | solution.py:119
  44.6 1.2 fusion.10
  45.7 5.0 %all-to-all-start = ((bf16[1,32,8,768]{3,2,0,1:T(8,128)(2,1)}), bf16[1,32,8,768]{3,2,0,1:T(8,128)(2,1)S(1)}, u32[]{:S(2)}, u32[]{:S(2)}) async-start(bf16[1,32,8,768]{3,2,0,1:T(8,128)(2,1)} %fusion.10), calls=%async_computation | async-start | bytes 786432 | tf_op jit(solution)/shard_map/all_to_all | solution.py:123
  50.8 0.7 constant_dynamic-update-slice_fusion.1
  51.5 1.6 copy.83
  53.1 1.1 reshape.613
  54.2 6.2 %all-to-all-done = bf16[1,32,8,768]{3,2,0,1:T(8,128)(2,1)S(1)} async-done(((bf16[1,32,8,768]{3,2,0,1:T(8,128)(2,1)}), bf16[1,32,8,768]{3,2,0,1:T(8,128)(2,1)S(1)}, u32[]{:S(2)}, u32[]{:S(2)}) %all-to-all-start) | async-done | bytes 393248 | tf_op jit(solution)/shard_map/all_to_all | solution.py:123
  60.4 0.9 reshape.608
  61.3 0.9 reshape.609
  62.3 2.1 fusion.164
  64.5 1.1 fusion.129
  65.5 2.0 fusion.14
  67.5 1.0 fusion.11
  68.6 2.6 %fusion.12 = bf16[1,8,32,4,64]{4,2,3,1,0:T(8,128)(2,1)} fusion(f32[8,4,32,32]{2,3,1,0:T(8,128)} %fusion.129, bf16[8,32,4,64]{3,2,1,0:T(4,128)(2,1)S(1)} %copy-done.18, f32[8,4,32,32]{2,3,1,0:T(8,128)} %get-tuple-element.147, f32[8,4,32]{2,1,0:T(4,128)S(1)} %get-tuple-element.146), kind=kOutput, calls=%fused_computation.20 | convolution fusion | flops 4490271 | bytes 528384 | tf_op jit(solution)/shard_map/brhqk,brkhd->brqhd/dot_general | solution.py:81
  71.2 1.1 copy.88
  72.3 0.9 convert_element_type.322
  73.2 1.1 copy.99
  74.3 0.9 reshape.619
  75.1 3.9 %all-to-all-start.1 = ((bf16[1,8,32,256]{3,1,0,2:T(8,128)(2,1)}), bf16[1,8,32,256]{3,1,0,2:T(8,128)(2,1)}, u32[]{:S(2)}, u32[]{:S(2)}) async-start(bf16[1,8,32,256]{3,1,0,2:T(8,128)(2,1)} %reshape.619), calls=%async_computation.1 | async-start | bytes 262144 | tf_op jit(solution)/shard_map/all_to_all | solution.py:131
  79.1 2.6 %fusion.13 = bf16[1,8,32,4,64]{4,2,3,1,0:T(8,128)(2,1)} fusion(f32[8,4,32,32]{2,3,1,0:T(8,128)} %fusion.129, bf16[8,32,4,64]{3,2,1,0:T(4,128)(2,1)S(1)} %copy-done.17, f32[8,4,32,32]{2,3,1,0:T(8,128)} %get-tuple-element.147, f32[8,4,32]{2,1,0:T(4,128)S(1)} %get-tuple-element.146), kind=kOutput, calls=%fused_computation.21 | convolution fusion | flops 4490271 | bytes 528384 | tf_op jit(solution)/shard_map/brhqk,brqhd->brkhd/dot_general | solution.py:84
  81.7 1.1 copy.90
  82.8 0.9 convert_element_type.326
  83.6 1.1 copy.92
  84.7 0.9 convert_element_type.330
  85.6 1.1 pad_maximum_fusion.2
  86.7 1.0 copy.93
  87.6 5.0 %all-to-all-start.3 = ((bf16[1,8,32,768]{3,1,0,2:T(8,128)(2,1)}), bf16[1,8,32,768]{3,1,0,2:T(8,128)(2,1)S(1)}, u32[]{:S(2)}, u32[]{:S(2)}) async-start(bf16[1,8,32,768]{3,1,0,2:T(8,128)(2,1)} %copy.93), calls=%async_computation.3 | async-start | bytes 786432 | tf_op jit(solution)/shard_map/all_to_all | solution.py:148
  92.7 1.7 constant_dynamic-update-slice_fusion
  94.3 0.9 copy.134
  95.3 1.0 fusion.122
  96.3 0.9 fusion.9
  97.3 4.3 %all-to-all-done.3 = bf16[1,8,32,768]{3,1,0,2:T(8,128)(2,1)S(1)} async-done(((bf16[1,8,32,768]{3,1,0,2:T(8,128)(2,1)}), bf16[1,8,32,768]{3,1,0,2:T(8,128)(2,1)S(1)}, u32[]{:S(2)}, u32[]{:S(2)}) %all-to-all-start.3) | async-done | bytes 393248 | tf_op jit(solution)/shard_map/all_to_all | solution.py:148
  101.7 1.0 multiply_reduce_fusion.1
  102.7 2.2 multiply_reduce_fusion.2
  104.9 2.0 multiply_reduce_fusion.29
  107.0 0.6 collective-permute-start.4
  107.6 3.3 %collective-permute-start.5 = (bf16[1,32,3,512]{3,2,1,0:T(4,128)(2,1)S(1)}, bf16[1,32,3,512]{3,2,1,0:T(4,128)(2,1)S(1)}, u32[]{:S(2)}, u32[]{:S(2)}) collective-permute-start(bf16[1,32,3,512]{3,2,1,0:T(4,128)(2,1)S(1)} %get-tuple-element.92), channel_id=1, source_target_pairs={{4,0},{8,4},{12,8},{0,12},{5,1},{9,5},{13,9},{1,13},{6,2},{10,6},{... | collective-permute-start | bytes 294920 | tf_op jit(solution)/shard_map/ppermute | solution.py:19
  110.9 1.7 multiply_reduce_fusion.20
  112.6 1.4 collective-permute-done.4
  114.1 1.9 collective-permute-start.6
  116.3 1.3 collective-permute-start.7
  117.6 1.6 fusion.139
  119.9 0.7 reshape.617
  120.9 0.3 copy-done.93
  121.2 31.5 %psum.31 = f32[512]{0:T(512)} all-reduce(f32[512]{0:T(512)S(1)} %copy-done.93), channel_id=1, replica_groups=mesh['member'=2,'lon'=4,'lat'=2,'dp'=2] {'lon','lat','dp'}, use_global_device_ids=true, to_apply=%region_58.0 | all-reduce | flops 512 | bytes 4096 | tf_op jit(solution)/shard_map/psum | solution.py:171
  153.3 4.5 %fusion.24 = bf16[1,32,8,512]{3,2,1,0:T(8,128)(2,1)} fusion(f32[1,32,8,512]{3,2,1,0:T(8,128)S(1)} %get-tuple-element.70, f32[1,38,14,512]{3,2,1,0:T(8,128)S(1)} %maximum_convert_fusion, f32[512]{0:T(512)S(1)} %bitcast.284, f32[512]{0:T(512)S(1)} %bitcast.286, f32[512]{0:T(512)S(1)} %bitcast.192, f32[512]{0:T(512)S(1)} %bitcast.194, f32[512]{0:T(512)S(1)} %bitcast.196, ...), kind=kLoop, calls=%fused_computation.42 | loop fusion | flops 12976128 | bytes 26576896 | tf_op jit(solution)/shard_map/convert_element_type | solution.py:169
  157.8 64.3 %all-reduce.3.cloned.1.call-done = (f32[512,768]{1,0:T(8,128)}, f32[256,512]{1,0:T(8,128)}, f32[7,7,512]{2,1,0:T(8,128)}) async-done(((f32[512,768]{1,0:T(8,128)}, f32[256,512]{1,0:T(8,128)}, f32[7,7,512]{2,1,0:T(8,128)}), (f32[512,768]{1,0:T(8,128)}, f32[256,512]{1,0:T(8,128)}, f32[7,7,512]{2,1,0:T(8,128)})) %all-reduce.3.cloned.1.call-update) | async-done | bytes 2197520 | tf_op jit(solution)/shard_map/psum | solution.py:171
  222.1 2.7 %copy.139 = f32[512,768]{1,0:T(8,128)} copy(f32[512,768]{1,0:T(8,128)} %get-tuple-element.154) | data formatting | bytes 3145728
  224.8 0.8 copy.140
  225.6 0.6 copy.141
  (212 shorter events, 1.5 us)
Async XLA Ops:
  7.2 37.4 %copy-start = (bf16[512,768]{1,0:T(8,128)(2,1)S(1)}, bf16[512,768]{1,0:T(8,128)(2,1)}, u32[]{:S(2)}) copy-start(bf16[512,768]{1,0:T(8,128)(2,1)} %param.10) | copy-start | bytes 2359300
  7.2 13.7 %copy-start.1 = (bf16[1,32,8,512]{3,2,1,0:T(8,128)(2,1)S(1)}, bf16[1,32,8,512]{3,2,1,0:T(8,128)(2,1)}, u32[]{:S(2)}) copy-start(bf16[1,32,8,512]{3,2,1,0:T(8,128)(2,1)} %param.6) | copy-start | bytes 786436
  7.2 12.3 %copy-start.20 = (f32[7,7,512]{2,1,0:T(8,128)S(1)}, f32[7,7,512]{2,1,0:T(8,128)}, u32[]{:S(2)}) copy-start(f32[7,7,512]{2,1,0:T(8,128)} %param.8) | copy-start | bytes 301060
  8.4 12.4 %collective-permute-start = (bf16[1,32,3,512]{3,2,1,0:T(4,128)(2,1)S(1)}, bf16[1,32,3,512]{3,2,1,0:T(4,128)(2,1)S(1)}, u32[]{:S(2)}, u32[]{:S(2)}) collective-permute-start(bf16[1,32,3,512]{3,2,1,0:T(4,128)(2,1)S(1)} %get-tuple-element.93), channel_id=1, source_target_pairs={{0,4},{4,8},{8,12},{12,0},{1,5},{5,9},{9,13},{13,1},{2,6},{6,10},{... | collective-permute-start | bytes 294920 | tf_op jit(solution)/shard_map/ppermute | solution.py:18
  11.6 9.3 %collective-permute-start.1 = (bf16[1,32,3,512]{3,2,1,0:T(4,128)(2,1)S(1)}, bf16[1,32,3,512]{3,2,1,0:T(4,128)(2,1)S(1)}, u32[]{:S(2)}, u32[]{:S(2)}) collective-permute-start(bf16[1,32,3,512]{3,2,1,0:T(4,128)(2,1)S(1)} %get-tuple-element.94), channel_id=1, source_target_pairs={{4,0},{8,4},{12,8},{0,12},{5,1},{9,5},{13,9},{1,13},{6,2},{10,6},{... | collective-permute-start | bytes 294920 | tf_op jit(solution)/shard_map/ppermute | solution.py:19
  15.6 30.2 %all-to-all-start.2 = ((bf16[1,32,8,256]{3,2,0,1:T(8,128)(2,1)}), bf16[1,32,8,256]{3,2,0,1:T(8,128)(2,1)}, u32[]{:S(2)}, u32[]{:S(2)}) async-start(bf16[1,32,8,256]{3,2,0,1:T(8,128)(2,1)} %fusion.15), calls=%async_computation.2 | async-start | bytes 262144 | tf_op jit(solution)/shard_map/all_to_all | solution.py:140
  20.8 11.2 %copy-start.8 = (bf16[1,32,3,512]{3,2,1,0:T(4,128)(2,1)}, bf16[1,32,3,512]{3,2,1,0:T(4,128)(2,1)S(1)}, u32[]{:S(2)}) copy-start(bf16[1,32,3,512]{3,2,1,0:T(4,128)(2,1)S(1)} %collective-permute-done) | copy-start | bytes 294916
  20.9 11.1 %copy-start.10 = (bf16[1,32,3,512]{3,2,1,0:T(4,128)(2,1)}, bf16[1,32,3,512]{3,2,1,0:T(4,128)(2,1)S(1)}, u32[]{:S(2)}) copy-start(bf16[1,32,3,512]{3,2,1,0:T(4,128)(2,1)S(1)} %collective-permute-done.1) | copy-start | bytes 294916
  22.1 5.5 %collective-permute-start.2 = (bf16[1,3,14,512]{3,2,1,0:T(8,128)(2,1)S(1)}, bf16[1,3,14,512]{3,2,1,0:T(8,128)(2,1)S(1)}, u32[]{:S(2)}, u32[]{:S(2)}) collective-permute-start(bf16[1,3,14,512]{3,2,1,0:T(8,128)(2,1)S(1)} %get-tuple-element.84), channel_id=1, source_target_pairs={{0,2},{1,3},{4,6},{5,7},{8,10},{9,11},{12,14},{13,15},{16,18},{17,... | collective-permute-start | bytes 129032 | tf_op jit(solution)/shard_map/ppermute | solution.py:18
  25.7 6.0 %collective-permute-start.3 = (bf16[1,3,14,512]{3,2,1,0:T(8,128)(2,1)S(1)}, bf16[1,3,14,512]{3,2,1,0:T(8,128)(2,1)S(1)}, u32[]{:S(2)}, u32[]{:S(2)}) collective-permute-start(bf16[1,3,14,512]{3,2,1,0:T(8,128)(2,1)S(1)} %get-tuple-element.85), channel_id=1, source_target_pairs={{2,0},{3,1},{6,4},{7,5},{10,8},{11,9},{14,12},{15,13},{18,16},{19,... | collective-permute-start | bytes 129032 | tf_op jit(solution)/shard_map/ppermute | solution.py:19
  34.0 10.5 %copy-start.21 = (f32[512]{0:T(512)S(1)}, f32[512]{0:T(512)}, u32[]{:S(2)}) copy-start(f32[512]{0:T(512)} %param.9) | copy-start | bytes 6148
  44.5 6.2 %copy-start.2 = (bf16[1,32,8,512]{3,2,1,0:T(8,128)(2,1)S(1)}, bf16[1,32,8,512]{3,2,1,0:T(8,128)(2,1)}, u32[]{:S(2)}) copy-start(bf16[1,32,8,512]{3,2,1,0:T(8,128)(2,1)} %param.6) | copy-start | bytes 786436
  45.7 14.6 %all-to-all-start = ((bf16[1,32,8,768]{3,2,0,1:T(8,128)(2,1)}), bf16[1,32,8,768]{3,2,0,1:T(8,128)(2,1)S(1)}, u32[]{:S(2)}, u32[]{:S(2)}) async-start(bf16[1,32,8,768]{3,2,0,1:T(8,128)(2,1)} %fusion.10), calls=%async_computation | async-start | bytes 786432 | tf_op jit(solution)/shard_map/all_to_all | solution.py:123
  71.2 7.9 %copy-start.17 = (bf16[8,32,4,64]{3,2,1,0:T(4,128)(2,1)S(1)}, bf16[8,32,4,64]{3,2,1,0:T(4,128)(2,1)}, u32[]{:S(2)}) copy-start(bf16[8,32,4,64]{3,2,1,0:T(4,128)(2,1)} %reshape.608) | copy-start | bytes 393220
  75.1 12.5 %all-to-all-start.1 = ((bf16[1,8,32,256]{3,1,0,2:T(8,128)(2,1)}), bf16[1,8,32,256]{3,1,0,2:T(8,128)(2,1)}, u32[]{:S(2)}, u32[]{:S(2)}) async-start(bf16[1,8,32,256]{3,1,0,2:T(8,128)(2,1)} %reshape.619), calls=%async_computation.1 | async-start | bytes 262144 | tf_op jit(solution)/shard_map/all_to_all | solution.py:131
  86.7 8.6 %copy-start.5 = (bf16[1,32,8,512]{3,2,1,0:T(8,128)(2,1)S(1)}, bf16[1,32,8,512]{3,2,1,0:T(8,128)(2,1)}, u32[]{:S(2)}) copy-start(bf16[1,32,8,512]{3,2,1,0:T(8,128)(2,1)} %param.7) | copy-start | bytes 786436
  87.6 13.9 %all-to-all-start.3 = ((bf16[1,8,32,768]{3,1,0,2:T(8,128)(2,1)}), bf16[1,8,32,768]{3,1,0,2:T(8,128)(2,1)S(1)}, u32[]{:S(2)}, u32[]{:S(2)}) async-start(bf16[1,8,32,768]{3,1,0,2:T(8,128)(2,1)} %copy.93), calls=%async_computation.3 | async-start | bytes 786432 | tf_op jit(solution)/shard_map/all_to_all | solution.py:148
  92.7 129.4 %all-reduce.3.cloned.1.call-start = ((), (), s32[]{:S(2)}) async-start(), calls=%async_computation.4 | async-start | bytes 4423680 | tf_op jit(solution)/shard_map/psum | solution.py:171
  104.9 6.0 %copy-start.7 = (bf16[1,32,11,512]{3,2,1,0:T(8,128)(2,1)S(1)}, bf16[1,32,11,512]{3,2,1,0:T(8,128)(2,1)}, u32[]{:S(2)}) copy-start(bf16[1,32,11,512]{3,2,1,0:T(8,128)(2,1)} %constant_dynamic-update-slice_fusion) | copy-start | bytes 1081348
  104.9 6.0 %copy-start.9 = (bf16[1,32,3,512]{3,2,1,0:T(4,128)(2,1)S(1)}, bf16[1,32,3,512]{3,2,1,0:T(4,128)(2,1)}, u32[]{:S(2)}) copy-start(bf16[1,32,3,512]{3,2,1,0:T(4,128)(2,1)} %copy-done.8) | copy-start | bytes 294916
  106.9 7.1 %copy-start.3 = (bf16[1,32,8,512]{3,2,1,0:T(8,128)(2,1)}, bf16[1,32,8,512]{3,2,1,0:T(8,128)(2,1)S(1)}, u32[]{:S(2)}) copy-start(bf16[1,32,8,512]{3,2,1,0:T(8,128)(2,1)S(1)} %get-tuple-element.79) | copy-start | bytes 786436
  107.0 6.9 %collective-permute-start.4 = (bf16[1,32,3,512]{3,2,1,0:T(4,128)(2,1)S(1)}, bf16[1,32,3,512]{3,2,1,0:T(4,128)(2,1)S(1)}, u32[]{:S(2)}, u32[]{:S(2)}) collective-permute-start(bf16[1,32,3,512]{3,2,1,0:T(4,128)(2,1)S(1)} %get-tuple-element.91), channel_id=1, source_target_pairs={{0,4},{4,8},{8,12},{12,0},{1,5},{5,9},{9,13},{13,1},{2,6},{6,10},{... | collective-permute-start | bytes 294920 | tf_op jit(solution)/shard_map/ppermute | solution.py:18
  107.6 6.4 %collective-permute-start.5 = (bf16[1,32,3,512]{3,2,1,0:T(4,128)(2,1)S(1)}, bf16[1,32,3,512]{3,2,1,0:T(4,128)(2,1)S(1)}, u32[]{:S(2)}, u32[]{:S(2)}) collective-permute-start(bf16[1,32,3,512]{3,2,1,0:T(4,128)(2,1)S(1)} %get-tuple-element.92), channel_id=1, source_target_pairs={{4,0},{8,4},{12,8},{0,12},{5,1},{9,5},{13,9},{1,13},{6,2},{10,6},{... | collective-permute-start | bytes 294920 | tf_op jit(solution)/shard_map/ppermute | solution.py:19
  114.1 38.6 %collective-permute-start.6 = (bf16[1,3,14,512]{3,2,1,0:T(8,128)(2,1)S(1)}, bf16[1,3,14,512]{3,2,1,0:T(8,128)(2,1)S(1)}, u32[]{:S(2)}, u32[]{:S(2)}) collective-permute-start(bf16[1,3,14,512]{3,2,1,0:T(8,128)(2,1)S(1)} %get-tuple-element.80), channel_id=1, source_target_pairs={{0,2},{1,3},{4,6},{5,7},{8,10},{9,11},{12,14},{13,15},{16,18},{17,... | collective-permute-start | bytes 129032 | tf_op jit(solution)/shard_map/ppermute | solution.py:18
  116.3 36.4 %collective-permute-start.7 = (bf16[1,3,14,512]{3,2,1,0:T(8,128)(2,1)S(1)}, bf16[1,3,14,512]{3,2,1,0:T(8,128)(2,1)S(1)}, u32[]{:S(2)}, u32[]{:S(2)}) collective-permute-start(bf16[1,3,14,512]{3,2,1,0:T(8,128)(2,1)S(1)} %get-tuple-element.81), channel_id=1, source_target_pairs={{2,0},{3,1},{6,4},{7,5},{10,8},{11,9},{14,12},{15,13},{18,16},{19,... | collective-permute-start | bytes 129032 | tf_op jit(solution)/shard_map/ppermute | solution.py:19
  119.8 32.8 %copy-start.4 = (bf16[1,32,8,512]{3,2,1,0:T(8,128)(2,1)S(1)}, bf16[1,32,8,512]{3,2,1,0:T(8,128)(2,1)}, u32[]{:S(2)}) copy-start(bf16[1,32,8,512]{3,2,1,0:T(8,128)(2,1)} %copy-done.3) | copy-start | bytes 786436
  119.8 32.8 %copy-start.13 = (bf16[1,32,3,512]{3,2,1,0:T(4,128)(2,1)S(1)}, bf16[1,32,3,512]{3,2,1,0:T(4,128)(2,1)}, u32[]{:S(2)}) copy-start(bf16[1,32,3,512]{3,2,1,0:T(4,128)(2,1)} %copy-done.12) | copy-start | bytes 294916
  119.8 32.8 %copy-start.15 = (bf16[1,32,3,512]{3,2,1,0:T(4,128)(2,1)S(1)}, bf16[1,32,3,512]{3,2,1,0:T(4,128)(2,1)}, u32[]{:S(2)}) copy-start(bf16[1,32,3,512]{3,2,1,0:T(4,128)(2,1)} %copy-done.14) | copy-start | bytes 294916
  120.5 32.4 %copy-start.22 = (f32[1,1,512]{2,1,0:T(1,128)S(1)}, f32[1,1,512]{2,1,0:T(1,128)}, u32[]{:S(2)}) copy-start(f32[1,1,512]{2,1,0:T(1,128)} %get-tuple-element.108) | copy-start | bytes 6148
  120.6 32.4 %copy-start.23 = (f32[1,1,512]{2,1,0:T(1,128)S(1)}, f32[1,1,512]{2,1,0:T(1,128)}, u32[]{:S(2)}) copy-start(f32[1,1,512]{2,1,0:T(1,128)} %get-tuple-element.109) | copy-start | bytes 6148
  120.6 32.4 %copy-start.24 = (f32[1,1,512]{2,1,0:T(1,128)S(1)}, f32[1,1,512]{2,1,0:T(1,128)}, u32[]{:S(2)}) copy-start(f32[1,1,512]{2,1,0:T(1,128)} %get-tuple-element.110) | copy-start | bytes 6148
  120.6 32.4 %copy-start.25 = (f32[1,1,512]{2,1,0:T(1,128)S(1)}, f32[1,1,512]{2,1,0:T(1,128)}, u32[]{:S(2)}) copy-start(f32[1,1,512]{2,1,0:T(1,128)} %get-tuple-element.111) | copy-start | bytes 6148
  120.6 32.4 %copy-start.26 = (f32[1,1,512]{2,1,0:T(1,128)S(1)}, f32[1,1,512]{2,1,0:T(1,128)}, u32[]{:S(2)}) copy-start(f32[1,1,512]{2,1,0:T(1,128)} %get-tuple-element.112) | copy-start | bytes 6148
  120.6 32.4 %copy-start.27 = (f32[1,1,512]{2,1,0:T(1,128)S(1)}, f32[1,1,512]{2,1,0:T(1,128)}, u32[]{:S(2)}) copy-start(f32[1,1,512]{2,1,0:T(1,128)} %get-tuple-element.113) | copy-start | bytes 6148
  120.6 32.4 %copy-start.28 = (f32[1,1,512]{2,1,0:T(1,128)S(1)}, f32[1,1,512]{2,1,0:T(1,128)}, u32[]{:S(2)}) copy-start(f32[1,1,512]{2,1,0:T(1,128)} %get-tuple-element.114) | copy-start | bytes 6148
  120.6 32.4 %copy-start.29 = (f32[1,1,512]{2,1,0:T(1,128)S(1)}, f32[1,1,512]{2,1,0:T(1,128)}, u32[]{:S(2)}) copy-start(f32[1,1,512]{2,1,0:T(1,128)} %get-tuple-element.115) | copy-start | bytes 6148
  120.6 32.4 %copy-start.30 = (f32[1,1,512]{2,1,0:T(1,128)S(1)}, f32[1,1,512]{2,1,0:T(1,128)}, u32[]{:S(2)}) copy-start(f32[1,1,512]{2,1,0:T(1,128)} %get-tuple-element.116) | copy-start | bytes 6148
  120.6 32.4 %copy-start.31 = (f32[1,1,512]{2,1,0:T(1,128)S(1)}, f32[1,1,512]{2,1,0:T(1,128)}, u32[]{:S(2)}) copy-start(f32[1,1,512]{2,1,0:T(1,128)} %get-tuple-element.117) | copy-start | bytes 6148
  120.6 32.4 %copy-start.32 = (f32[1,1,512]{2,1,0:T(1,128)S(1)}, f32[1,1,512]{2,1,0:T(1,128)}, u32[]{:S(2)}) copy-start(f32[1,1,512]{2,1,0:T(1,128)} %get-tuple-element.118) | copy-start | bytes 6148
  120.7 32.4 %copy-start.33 = (f32[1,1,512]{2,1,0:T(1,128)S(1)}, f32[1,1,512]{2,1,0:T(1,128)}, u32[]{:S(2)}) copy-start(f32[1,1,512]{2,1,0:T(1,128)} %get-tuple-element.119) | copy-start | bytes 6148
  120.7 32.4 %copy-start.34 = (f32[1,1,512]{2,1,0:T(1,128)S(1)}, f32[1,1,512]{2,1,0:T(1,128)}, u32[]{:S(2)}) copy-start(f32[1,1,512]{2,1,0:T(1,128)} %get-tuple-element.120) | copy-start | bytes 6148
  120.7 32.4 %copy-start.35 = (f32[1,1,512]{2,1,0:T(1,128)S(1)}, f32[1,1,512]{2,1,0:T(1,128)}, u32[]{:S(2)}) copy-start(f32[1,1,512]{2,1,0:T(1,128)} %get-tuple-element.121) | copy-start | bytes 6148
  120.7 32.4 %copy-start.36 = (f32[1,1,512]{2,1,0:T(1,128)S(1)}, f32[1,1,512]{2,1,0:T(1,128)}, u32[]{:S(2)}) copy-start(f32[1,1,512]{2,1,0:T(1,128)} %get-tuple-element.122) | copy-start | bytes 6148
  120.7 32.4 %copy-start.37 = (f32[1,1,512]{2,1,0:T(1,128)S(1)}, f32[1,1,512]{2,1,0:T(1,128)}, u32[]{:S(2)}) copy-start(f32[1,1,512]{2,1,0:T(1,128)} %get-tuple-element.123) | copy-start | bytes 6148
  120.7 32.4 %copy-start.38 = (f32[1,1,512]{2,1,0:T(1,128)S(1)}, f32[1,1,512]{2,1,0:T(1,128)}, u32[]{:S(2)}) copy-start(f32[1,1,512]{2,1,0:T(1,128)} %get-tuple-element.124) | copy-start | bytes 6148
  120.7 32.4 %copy-start.39 = (f32[1,1,512]{2,1,0:T(1,128)S(1)}, f32[1,1,512]{2,1,0:T(1,128)}, u32[]{:S(2)}) copy-start(f32[1,1,512]{2,1,0:T(1,128)} %get-tuple-element.125) | copy-start | bytes 6148
  120.7 32.4 %copy-start.40 = (f32[1,1,512]{2,1,0:T(1,128)S(1)}, f32[1,1,512]{2,1,0:T(1,128)}, u32[]{:S(2)}) copy-start(f32[1,1,512]{2,1,0:T(1,128)} %get-tuple-element.126) | copy-start | bytes 6148
  120.7 32.4 %copy-start.41 = (f32[1,1,512]{2,1,0:T(1,128)S(1)}, f32[1,1,512]{2,1,0:T(1,128)}, u32[]{:S(2)}) copy-start(f32[1,1,512]{2,1,0:T(1,128)} %get-tuple-element.127) | copy-start | bytes 6148
  120.7 32.4 %copy-start.42 = (f32[1,1,512]{2,1,0:T(1,128)S(1)}, f32[1,1,512]{2,1,0:T(1,128)}, u32[]{:S(2)}) copy-start(f32[1,1,512]{2,1,0:T(1,128)} %get-tuple-element.128) | copy-start | bytes 6148
  120.8 32.4 %copy-start.43 = (f32[1,1,512]{2,1,0:T(1,128)S(1)}, f32[1,1,512]{2,1,0:T(1,128)}, u32[]{:S(2)}) copy-start(f32[1,1,512]{2,1,0:T(1,128)} %get-tuple-element.129) | copy-start | bytes 6148
  120.8 32.4 %copy-start.44 = (f32[1,1,512]{2,1,0:T(1,128)S(1)}, f32[1,1,512]{2,1,0:T(1,128)}, u32[]{:S(2)}) copy-start(f32[1,1,512]{2,1,0:T(1,128)} %get-tuple-element.130) | copy-start | bytes 6148
  120.8 32.4 %copy-start.45 = (f32[1,1,512]{2,1,0:T(1,128)S(1)}, f32[1,1,512]{2,1,0:T(1,128)}, u32[]{:S(2)}) copy-start(f32[1,1,512]{2,1,0:T(1,128)} %get-tuple-element.131) | copy-start | bytes 6148
  120.8 32.4 %copy-start.46 = (f32[1,1,512]{2,1,0:T(1,128)S(1)}, f32[1,1,512]{2,1,0:T(1,128)}, u32[]{:S(2)}) copy-start(f32[1,1,512]{2,1,0:T(1,128)} %get-tuple-element.132) | copy-start | bytes 6148
  120.8 32.4 %copy-start.47 = (f32[1,1,512]{2,1,0:T(1,128)S(1)}, f32[1,1,512]{2,1,0:T(1,128)}, u32[]{:S(2)}) copy-start(f32[1,1,512]{2,1,0:T(1,128)} %get-tuple-element.133) | copy-start | bytes 6148
  120.8 32.4 %copy-start.48 = (f32[1,1,512]{2,1,0:T(1,128)S(1)}, f32[1,1,512]{2,1,0:T(1,128)}, u32[]{:S(2)}) copy-start(f32[1,1,512]{2,1,0:T(1,128)} %get-tuple-element.134) | copy-start | bytes 6148
  120.8 32.4 %copy-start.49 = (f32[1,1,512]{2,1,0:T(1,128)S(1)}, f32[1,1,512]{2,1,0:T(1,128)}, u32[]{:S(2)}) copy-start(f32[1,1,512]{2,1,0:T(1,128)} %get-tuple-element.135) | copy-start | bytes 6148
  120.8 32.4 %copy-start.50 = (f32[1,1,512]{2,1,0:T(1,128)S(1)}, f32[1,1,512]{2,1,0:T(1,128)}, u32[]{:S(2)}) copy-start(f32[1,1,512]{2,1,0:T(1,128)} %get-tuple-element.136) | copy-start | bytes 6148
  120.8 32.4 %copy-start.51 = (f32[1,1,512]{2,1,0:T(1,128)S(1)}, f32[1,1,512]{2,1,0:T(1,128)}, u32[]{:S(2)}) copy-start(f32[1,1,512]{2,1,0:T(1,128)} %get-tuple-element.137) | copy-start | bytes 6148
  120.8 32.4 %copy-start.52 = (f32[1,1,512]{2,1,0:T(1,128)S(1)}, f32[1,1,512]{2,1,0:T(1,128)}, u32[]{:S(2)}) copy-start(f32[1,1,512]{2,1,0:T(1,128)} %get-tuple-element.138) | copy-start | bytes 6148
  120.9 32.4 %copy-start.53 = (f32[1,1,512]{2,1,0:T(1,128)S(1)}, f32[1,1,512]{2,1,0:T(1,128)}, u32[]{:S(2)}) copy-start(f32[1,1,512]{2,1,0:T(1,128)} %get-tuple-element.139) | copy-start | bytes 6148
  120.9 32.4 %copy-start.54 = (f32[1,1,512]{2,1,0:T(1,128)S(1)}, f32[1,1,512]{2,1,0:T(1,128)}, u32[]{:S(2)}) copy-start(f32[1,1,512]{2,1,0:T(1,128)} %get-tuple-element.140) | copy-start | bytes 6148
  120.9 32.4 %copy-start.55 = (f32[1,1,512]{2,1,0:T(1,128)S(1)}, f32[1,1,512]{2,1,0:T(1,128)}, u32[]{:S(2)}) copy-start(f32[1,1,512]{2,1,0:T(1,128)} %get-tuple-element.141) | copy-start | bytes 6148
  120.9 32.4 %copy-start.56 = (f32[1,1,512]{2,1,0:T(1,128)S(1)}, f32[1,1,512]{2,1,0:T(1,128)}, u32[]{:S(2)}) copy-start(f32[1,1,512]{2,1,0:T(1,128)} %get-tuple-element.142) | copy-start | bytes 6148
  120.9 32.4 %copy-start.57 = (f32[1,1,512]{2,1,0:T(1,128)S(1)}, f32[1,1,512]{2,1,0:T(1,128)}, u32[]{:S(2)}) copy-start(f32[1,1,512]{2,1,0:T(1,128)} %get-tuple-element.143) | copy-start | bytes 6148
  (44 other events, 140.4 us)
Sparse Core Ops, SparseCore 0:
  120.7 101.3 all-reduce.2
where the time goes:
time: 234 us; the launch traced here: 233 us
  waiting for transfers between devices  80.2 us (34%)
  starting transfers between devices  35 us (15%)
  blocking collectives  31.5 us (13%)
  local copies, waits for them, and re-layouts  25.9 us (11%)
  other arithmetic  25.8 us (11%)
  matrix products  19.2 us (8%)
  between operations  15.5 us (7%)
    psum x1, waiting for transfers between devices, on_device(): lax.psum((grad_weight, grad_out, grad_conv, grad_gain), ('lon', 'lat', 'd...  64.3 us
    psum x1, blocking collectives, on_device(): lax.psum((grad_weight, grad_out, grad_conv, grad_gain), ('lon', 'lat', 'd...  31.5 us
    reduce_sum x1, other arithmetic, on_device(): inverse = lax.rsqrt(jnp.mean(update * update, -1, keepdims=True) + EPSILON)  10.5 us
    ppermute x4, starting transfers between devices, with_halo(): before = lax.ppermute(last, axis, up)  9.14 us
    ppermute x4, starting transfers between devices, with_halo(): after = lax.ppermute(first, axis, down)  7.95 us
    all_to_all x1, waiting for transfers between devices, on_device(): lax.all_to_all(projected.reshape(batch_count, lat_rows, lon_cols, 3 * att...  6.17 us
    reduce_sum x3, other arithmetic, correlate(): pieces.append(jnp.sum(window * upstream, axis=(0, 1, 2)))  5.91 us
    unnamed x194, local copies, waits for them, and re-layouts  5.57 us
  transfers between devices with their start and end apart: 13, of which 6 were waited for; matrix products, arithmetic and copies ran while one was open for 19% of the time, Pallas kernels for 0%

commit v1 on v0

--- a/solution.py
+++ b/solution.py
@@ -168,7 +168,8 @@
         grad_update + spread(grad_padded, conv_weight[::-1, ::-1], lat_rows, lon_cols)
     ).astype(jnp.bfloat16)
     grad_conv = correlate(padded, grad_update, lat_rows, lon_cols)
-    totals = lax.psum((grad_weight, grad_out, grad_conv, grad_gain), ("lon", "lat", "dp"))
+    one_axis = lax.psum((grad_weight, grad_out, grad_conv, grad_gain), ("lat", "dp"))
+    totals = lax.psum(one_axis, "lon")
     return (result, grad_fields, totals[0], totals[1], totals[2], totals[3])
 
 

time: 234 us -> 270 us (1.15)
  waiting for transfers between devices: 80.2 us -> 129 us
  blocking collectives: 31.5 us -> 18.8 us
    psum x1 -> x2, waiting for transfers between devices: 64.3 us -> 106 us  [the longest x1 53.9 us: on_device(): totals = lax.psum(one_axis, 'lon')]
    psum x1 -> x2, blocking collectives: 31.5 us -> 18.8 us  [the longest x1 11.6 us: on_device(): totals = lax.psum(one_axis, 'lon')]
    another operation x1, local copies, waits for them, and re-layouts: 0.24 us -> 3.78 us  [correlate(): return jnp.stack(pieces).reshape(7, 7, -1)]
    ppermute x4, waiting for transfers between devices: 1.36 us -> 4.36 us  [with_halo(): before = lax.ppermute(last, axis, up)]
    unnamed x194 -> x166, local copies, waits for them, and re-layouts: 5.57 us -> 5.17 us
  transfers between devices with their start and end apart: 13 -> 14, of which waited for: 6 -> 7; matrix products, arithmetic and copies ran while one was open for 19% -> 13% of each run, Pallas kernels for 0% -> 0%
where the time goes in v1:
time: 270 us; the launch traced here: 268 us
  waiting for transfers between devices  129 us (48%)
  starting transfers between devices  35.8 us (13%)
  other arithmetic  25.4 us (9%)
  local copies, waits for them, and re-layouts  25.2 us (9%)
  matrix products  19.3 us (7%)
  blocking collectives  18.8 us (7%)
  between operations  15.3 us (6%)
    psum x1, waiting for transfers between devices, on_device(): totals = lax.psum(one_axis, 'lon')  53.9 us
    psum x1, waiting for transfers between devices, on_device(): lax.psum((grad_weight, grad_out, grad_conv, grad_gain), ('lat', 'dp'))  51.7 us
    psum x1, blocking collectives, on_device(): totals = lax.psum(one_axis, 'lon')  11.6 us
    ppermute x4, starting transfers between devices, with_halo(): before = lax.ppermute(last, axis, up)  10.7 us
    reduce_sum x1, other arithmetic, on_device(): inverse = lax.rsqrt(jnp.mean(update * update, -1, keepdims=True) + EPSILON)  10.5 us
    all_to_all x1, waiting for transfers between devices, on_device(): lax.all_to_all(projected.reshape(batch_count, lat_rows, lon_cols, 3 * att...  8.46 us
    psum x1, blocking collectives, on_device(): lax.psum((grad_weight, grad_out, grad_conv, grad_gain), ('lat', 'dp'))  7.28 us
    ppermute x4, starting transfers between devices, with_halo(): after = lax.ppermute(first, axis, down)  7.01 us
  transfers between devices with their start and end apart: 14, of which 7 were waited for; matrix products, arithmetic and copies ran while one was open for 13% of the time, Pallas kernels for 0%

profile of v1, /device:TPU:0, one launch (start us, length us, event | category | flops | bytes accessed | tf_op | source)
XLA Modules:
  0.0 268.5 jit_solution(944813852257778223)
XLA Ops:
  7.2 1.2 fusion.160
  8.4 3.1 %collective-permute-start = (bf16[1,32,3,512]{3,2,1,0:T(4,128)(2,1)S(1)}, bf16[1,32,3,512]{3,2,1,0:T(4,128)(2,1)S(1)}, u32[]{:S(2)}, u32[]{:S(2)}) collective-permute-start(bf16[1,32,3,512]{3,2,1,0:T(4,128)(2,1)S(1)} %get-tuple-element.96), channel_id=1, source_target_pairs={{0,4},{4,8},{8,12},{12,0},{1,5},{5,9},{9,13},{13,1},{2,6},{6,10},{... | collective-permute-start | bytes 294920 | tf_op jit(solution)/shard_map/ppermute | solution.py:18
  11.6 2.1 collective-permute-start.1
  13.6 1.9 fusion.15
  15.6 3.9 %all-to-all-start.2 = ((bf16[1,32,8,256]{3,2,0,1:T(8,128)(2,1)}), bf16[1,32,8,256]{3,2,0,1:T(8,128)(2,1)}, u32[]{:S(2)}, u32[]{:S(2)}) async-start(bf16[1,32,8,256]{3,2,0,1:T(8,128)(2,1)} %fusion.15), calls=%async_computation.2 | async-start | bytes 262144 | tf_op jit(solution)/shard_map/all_to_all | solution.py:140
  19.6 0.6 fusion.161
  20.3 0.7 fusion.162
  21.0 1.2 fusion.156
  22.2 3.5 %collective-permute-start.2 = (bf16[1,3,14,512]{3,2,1,0:T(8,128)(2,1)S(1)}, bf16[1,3,14,512]{3,2,1,0:T(8,128)(2,1)S(1)}, u32[]{:S(2)}, u32[]{:S(2)}) collective-permute-start(bf16[1,3,14,512]{3,2,1,0:T(8,128)(2,1)S(1)} %get-tuple-element.87), channel_id=1, source_target_pairs={{0,2},{1,3},{4,6},{5,7},{8,10},{9,11},{12,14},{13,15},{16,18},{17,... | collective-permute-start | bytes 129032 | tf_op jit(solution)/shard_map/ppermute | solution.py:18
  25.8 1.3 collective-permute-start.3
  27.1 0.6 fusion.163
  27.7 4.0 %collective-permute-done.3 = bf16[1,3,14,512]{3,2,1,0:T(8,128)(2,1)S(1)} collective-permute-done((bf16[1,3,14,512]{3,2,1,0:T(8,128)(2,1)S(1)}, bf16[1,3,14,512]{3,2,1,0:T(8,128)(2,1)S(1)}, u32[]{:S(2)}, u32[]{:S(2)}) %collective-permute-start.3) | collective-permute-done | bytes 43040 | tf_op jit(solution)/shard_map/ppermute | solution.py:19
  31.8 0.3 maximum_maximum_fusion
  32.1 1.9 slice_convert_fusion.2
  34.1 10.5 %multiply_reduce_fusion.51 = (f32[32,8]{1,0:T(8,128)S(1)}, f32[1,32,8,512]{3,2,1,0:T(8,128)S(1)}) fusion(f32[1,32,14,512]{3,2,1,0:T(8,128)S(1)} %get-tuple-element.80, f32[512]{0:T(512)} %bitcast.283, f32[512]{0:T(512)} %bitcast.285, f32[512]{0:T(512)S(1)} %bitcast.191, f32[512]{0:T(512)S(1)} %bitcast.193, f32[512]{0:T(512)S(1)} %bitcast.195, ...), kind=kLoop, calls=%fused_computation.293 | loop fusion | flops 13238016 | bytes 26577920 | tf_op jit(solution)/shard_map/reduce_sum | solution.py:119
  44.7 1.2 fusion.10
  45.8 5.0 %all-to-all-start = ((bf16[1,32,8,768]{3,2,0,1:T(8,128)(2,1)}), bf16[1,32,8,768]{3,2,0,1:T(8,128)(2,1)S(1)}, u32[]{:S(2)}, u32[]{:S(2)}) async-start(bf16[1,32,8,768]{3,2,0,1:T(8,128)(2,1)} %fusion.10), calls=%async_computation | async-start | bytes 786432 | tf_op jit(solution)/shard_map/all_to_all | solution.py:123
  50.9 0.9 copy.83
  51.9 8.5 %all-to-all-done = bf16[1,32,8,768]{3,2,0,1:T(8,128)(2,1)S(1)} async-done(((bf16[1,32,8,768]{3,2,0,1:T(8,128)(2,1)}), bf16[1,32,8,768]{3,2,0,1:T(8,128)(2,1)S(1)}, u32[]{:S(2)}, u32[]{:S(2)}) %all-to-all-start) | async-done | bytes 393248 | tf_op jit(solution)/shard_map/all_to_all | solution.py:123
  60.7 0.9 reshape.609
  61.7 2.1 fusion.164
  63.8 1.1 fusion.129
  64.8 2.0 fusion.14
  66.8 1.8 fusion.11
  68.6 2.3 fusion.12
  70.9 1.1 copy.88
  72.0 0.2 convert_element_type.322
  72.2 1.1 copy.99
  73.3 0.9 reshape.619
  74.2 3.9 %all-to-all-start.1 = ((bf16[1,8,32,256]{3,1,0,2:T(8,128)(2,1)}), bf16[1,8,32,256]{3,1,0,2:T(8,128)(2,1)}, u32[]{:S(2)}, u32[]{:S(2)}) async-start(bf16[1,8,32,256]{3,1,0,2:T(8,128)(2,1)} %reshape.619), calls=%async_computation.1 | async-start | bytes 262144 | tf_op jit(solution)/shard_map/all_to_all | solution.py:131
  78.2 2.3 fusion.13
  80.5 1.1 copy.90
  81.8 1.1 copy.92
  83.1 1.0 copy.93
  84.1 5.1 %all-to-all-start.3 = ((bf16[1,8,32,768]{3,1,0,2:T(8,128)(2,1)}), bf16[1,8,32,768]{3,1,0,2:T(8,128)(2,1)}, u32[]{:S(2)}, u32[]{:S(2)}) async-start(bf16[1,8,32,768]{3,1,0,2:T(8,128)(2,1)} %copy.93), calls=%async_computation.3 | async-start | bytes 786432 | tf_op jit(solution)/shard_map/all_to_all | solution.py:148
  89.3 1.0 constant_dynamic-update-slice_fusion
  90.3 1.1 copy.134
  91.4 0.6 copy-done.9
  92.1 1.0 fusion.122
  93.1 5.1 %all-to-all-done.3 = bf16[1,8,32,768]{3,1,0,2:T(8,128)(2,1)} async-done(((bf16[1,8,32,768]{3,1,0,2:T(8,128)(2,1)}), bf16[1,8,32,768]{3,1,0,2:T(8,128)(2,1)}, u32[]{:S(2)}, u32[]{:S(2)}) %all-to-all-start.3) | async-done | bytes 393248 | tf_op jit(solution)/shard_map/all_to_all | solution.py:148
  98.3 1.1 copy.132
  99.4 1.0 multiply_reduce_fusion.1
  100.4 1.6 fusion.139
  102.0 2.3 multiply_reduce_fusion.2
  104.3 2.0 multiply_reduce_fusion.29
  106.4 1.7 multiply_reduce_fusion.20
  108.1 3.8 %stack.199 = f32[49,512]{1,0:T(8,128)S(1)} concatenate(f32[1,512]{1,0:T(1,128)} %bitcast.333, f32[1,512]{1,0:T(1,128)} %bitcast.334, f32[1,512]{1,0:T(1,128)} %bitcast.335, f32[1,512]{1,0:T(1,128)} %bitcast.322, f32[1,512]{1,0:T(1,128)} %bitcast.321, f32[1,512]{1,0:T(1,128)} %bitcast.320, f32[1,512]{1,0:T(1,128)} %bitcast.319, f32[1,512]{1,0:T(1,128)} %bitcast.318, ...), dimensions={0} | concatenate | bytes 200704 | tf_op jit(solution)/shard_map/stack | solution.py:46
  111.9 0.7 reshape.617
  112.7 51.7 %all-reduce.5.cloned.1.call-done = (f32[512,768]{1,0:T(8,128)}, f32[256,512]{1,0:T(8,128)}, f32[7,7,512]{2,1,0:T(8,128)}) async-done(((f32[512,768]{1,0:T(8,128)}, f32[256,512]{1,0:T(8,128)}, f32[7,7,512]{2,1,0:T(8,128)}), (f32[512,768]{1,0:T(8,128)}, f32[256,512]{1,0:T(8,128)}, f32[7,7,512]{2,1,0:T(8,128)})) %all-reduce.5.cloned.1.call-update) | async-done | bytes 2197520 | tf_op jit(solution)/shard_map/psum | solution.py:171
  164.5 1.5 collective-permute-start.4
  166.1 2.3 collective-permute-start.5
  168.4 4.4 %collective-permute-done.4 = bf16[1,32,3,512]{3,2,1,0:T(4,128)(2,1)S(1)} collective-permute-done((bf16[1,32,3,512]{3,2,1,0:T(4,128)(2,1)S(1)}, bf16[1,32,3,512]{3,2,1,0:T(4,128)(2,1)S(1)}, u32[]{:S(2)}, u32[]{:S(2)}) %collective-permute-start.4) | collective-permute-done | bytes 98336 | tf_op jit(solution)/shard_map/ppermute | solution.py:18
  172.8 0.9 collective-permute-done.5
  173.7 2.5 collective-permute-start.6
  176.3 1.3 collective-permute-start.7
  178.0 0.9 fusion.9
  178.9 7.3 %psum.62 = f32[512]{0:T(512)S(1)} all-reduce(f32[512]{0:T(512)} %get-tuple-element.48), channel_id=1, replica_groups=mesh['member'=2,'lon'=4,'lat'=2,'dp'=2] {'lat','dp'}, use_global_device_ids=true, to_apply=%region_61.0 | all-reduce | flops 512 | bytes 4096 | tf_op jit(solution)/shard_map/psum | solution.py:171
  186.2 11.6 %psum.63 = f32[512]{0:T(512)} all-reduce(f32[512]{0:T(512)S(1)} %psum.62), channel_id=1, replica_groups=mesh['member'=2,'lon'=4,'lat'=2,'dp'=2] {'lon'}, use_global_device_ids=true, to_apply=%region_62.0 | all-reduce | flops 512 | bytes 4096 | tf_op jit(solution)/shard_map/psum | solution.py:172
  197.8 0.2 maximum_convert_fusion
  198.4 5.2 %fusion.24 = bf16[1,32,8,512]{3,2,1,0:T(8,128)(2,1)} fusion(f32[1,32,8,512]{3,2,1,0:T(8,128)S(1)} %get-tuple-element.73, f32[1,38,14,512]{3,2,1,0:T(8,128)S(1)} %maximum_convert_fusion, f32[512]{0:T(512)} %bitcast.284, f32[512]{0:T(512)} %bitcast.286, f32[512]{0:T(512)S(1)} %bitcast.192, f32[512]{0:T(512)S(1)} %bitcast.194, f32[512]{0:T(512)S(1)} %bitcast.196, ...), kind=kLoop, calls=%fused_computation.42 | loop fusion | flops 12976128 | bytes 26576896 | tf_op jit(solution)/shard_map/convert_element_type | solution.py:169
  203.6 53.9 %all-reduce.7.cloned.1.call-done = (f32[512,768]{1,0:T(8,128)}, f32[256,512]{1,0:T(8,128)}, f32[7,7,512]{2,1,0:T(8,128)}) async-done(((f32[512,768]{1,0:T(8,128)}, f32[256,512]{1,0:T(8,128)}, f32[7,7,512]{2,1,0:T(8,128)}), (f32[512,768]{1,0:T(8,128)}, f32[256,512]{1,0:T(8,128)}, f32[7,7,512]{2,1,0:T(8,128)})) %all-reduce.7.cloned.1.call-update) | async-done | bytes 2197520 | tf_op jit(solution)/shard_map/psum | solution.py:172
  257.5 2.7 %copy.142 = f32[512,768]{1,0:T(8,128)} copy(f32[512,768]{1,0:T(8,128)} %get-tuple-element.157) | data formatting | bytes 3145728
  260.2 0.8 copy.143
  261.0 0.6 copy.144
  (188 shorter events, 1.7 us)
Async XLA Ops:
  7.2 37.5 %copy-start = (bf16[512,768]{1,0:T(8,128)(2,1)S(1)}, bf16[512,768]{1,0:T(8,128)(2,1)}, u32[]{:S(2)}) copy-start(bf16[512,768]{1,0:T(8,128)(2,1)} %param.10) | copy-start | bytes 2359300
  8.4 12.5 %collective-permute-start = (bf16[1,32,3,512]{3,2,1,0:T(4,128)(2,1)S(1)}, bf16[1,32,3,512]{3,2,1,0:T(4,128)(2,1)S(1)}, u32[]{:S(2)}, u32[]{:S(2)}) collective-permute-start(bf16[1,32,3,512]{3,2,1,0:T(4,128)(2,1)S(1)} %get-tuple-element.96), channel_id=1, source_target_pairs={{0,4},{4,8},{8,12},{12,0},{1,5},{5,9},{9,13},{13,1},{2,6},{6,10},{... | collective-permute-start | bytes 294920 | tf_op jit(solution)/shard_map/ppermute | solution.py:18
  11.6 9.4 %collective-permute-start.1 = (bf16[1,32,3,512]{3,2,1,0:T(4,128)(2,1)S(1)}, bf16[1,32,3,512]{3,2,1,0:T(4,128)(2,1)S(1)}, u32[]{:S(2)}, u32[]{:S(2)}) collective-permute-start(bf16[1,32,3,512]{3,2,1,0:T(4,128)(2,1)S(1)} %get-tuple-element.97), channel_id=1, source_target_pairs={{4,0},{8,4},{12,8},{0,12},{5,1},{9,5},{13,9},{1,13},{6,2},{10,6},{... | collective-permute-start | bytes 294920 | tf_op jit(solution)/shard_map/ppermute | solution.py:19
  15.6 30.2 %all-to-all-start.2 = ((bf16[1,32,8,256]{3,2,0,1:T(8,128)(2,1)}), bf16[1,32,8,256]{3,2,0,1:T(8,128)(2,1)}, u32[]{:S(2)}, u32[]{:S(2)}) async-start(bf16[1,32,8,256]{3,2,0,1:T(8,128)(2,1)} %fusion.15), calls=%async_computation.2 | async-start | bytes 262144 | tf_op jit(solution)/shard_map/all_to_all | solution.py:140
  20.2 13.8 %copy-start.19 = (f32[1,1,512]{2,1,0:T(1,128)}, f32[1,1,512]{2,1,0:T(1,128)S(1)}, u32[]{:S(2)}) copy-start(f32[1,1,512]{2,1,0:T(1,128)S(1)} %get-tuple-element.101) | copy-start | bytes 6148
  20.2 13.8 %copy-start.21 = (f32[1,1,512]{2,1,0:T(1,128)}, f32[1,1,512]{2,1,0:T(1,128)S(1)}, u32[]{:S(2)}) copy-start(f32[1,1,512]{2,1,0:T(1,128)S(1)} %get-tuple-element.102) | copy-start | bytes 6148
  20.2 13.8 %copy-start.23 = (f32[1,1,512]{2,1,0:T(1,128)}, f32[1,1,512]{2,1,0:T(1,128)S(1)}, u32[]{:S(2)}) copy-start(f32[1,1,512]{2,1,0:T(1,128)S(1)} %get-tuple-element.103) | copy-start | bytes 6148
  20.2 13.8 %copy-start.25 = (f32[1,1,512]{2,1,0:T(1,128)}, f32[1,1,512]{2,1,0:T(1,128)S(1)}, u32[]{:S(2)}) copy-start(f32[1,1,512]{2,1,0:T(1,128)S(1)} %get-tuple-element.104) | copy-start | bytes 6148
  20.2 13.8 %copy-start.27 = (f32[1,1,512]{2,1,0:T(1,128)}, f32[1,1,512]{2,1,0:T(1,128)S(1)}, u32[]{:S(2)}) copy-start(f32[1,1,512]{2,1,0:T(1,128)S(1)} %get-tuple-element.105) | copy-start | bytes 6148
  20.2 13.8 %copy-start.29 = (f32[1,1,512]{2,1,0:T(1,128)}, f32[1,1,512]{2,1,0:T(1,128)S(1)}, u32[]{:S(2)}) copy-start(f32[1,1,512]{2,1,0:T(1,128)S(1)} %get-tuple-element.106) | copy-start | bytes 6148
  20.2 13.8 %copy-start.31 = (f32[1,1,512]{2,1,0:T(1,128)}, f32[1,1,512]{2,1,0:T(1,128)S(1)}, u32[]{:S(2)}) copy-start(f32[1,1,512]{2,1,0:T(1,128)S(1)} %get-tuple-element.107) | copy-start | bytes 6148
  20.2 13.8 %copy-start.33 = (f32[1,1,512]{2,1,0:T(1,128)}, f32[1,1,512]{2,1,0:T(1,128)S(1)}, u32[]{:S(2)}) copy-start(f32[1,1,512]{2,1,0:T(1,128)S(1)} %get-tuple-element.108) | copy-start | bytes 6148
  20.2 13.8 %copy-start.35 = (f32[1,1,512]{2,1,0:T(1,128)}, f32[1,1,512]{2,1,0:T(1,128)S(1)}, u32[]{:S(2)}) copy-start(f32[1,1,512]{2,1,0:T(1,128)S(1)} %get-tuple-element.109) | copy-start | bytes 6148
  22.2 5.5 %collective-permute-start.2 = (bf16[1,3,14,512]{3,2,1,0:T(8,128)(2,1)S(1)}, bf16[1,3,14,512]{3,2,1,0:T(8,128)(2,1)S(1)}, u32[]{:S(2)}, u32[]{:S(2)}) collective-permute-start(bf16[1,3,14,512]{3,2,1,0:T(8,128)(2,1)S(1)} %get-tuple-element.87), channel_id=1, source_target_pairs={{0,2},{1,3},{4,6},{5,7},{8,10},{9,11},{12,14},{13,15},{16,18},{17,... | collective-permute-start | bytes 129032 | tf_op jit(solution)/shard_map/ppermute | solution.py:18
  25.8 6.0 %collective-permute-start.3 = (bf16[1,3,14,512]{3,2,1,0:T(8,128)(2,1)S(1)}, bf16[1,3,14,512]{3,2,1,0:T(8,128)(2,1)S(1)}, u32[]{:S(2)}, u32[]{:S(2)}) collective-permute-start(bf16[1,3,14,512]{3,2,1,0:T(8,128)(2,1)S(1)} %get-tuple-element.88), channel_id=1, source_target_pairs={{2,0},{3,1},{6,4},{7,5},{10,8},{11,9},{14,12},{15,13},{18,16},{19,... | collective-permute-start | bytes 129032 | tf_op jit(solution)/shard_map/ppermute | solution.py:19
  45.8 14.6 %all-to-all-start = ((bf16[1,32,8,768]{3,2,0,1:T(8,128)(2,1)}), bf16[1,32,8,768]{3,2,0,1:T(8,128)(2,1)S(1)}, u32[]{:S(2)}, u32[]{:S(2)}) async-start(bf16[1,32,8,768]{3,2,0,1:T(8,128)(2,1)} %fusion.10), calls=%async_computation | async-start | bytes 786432 | tf_op jit(solution)/shard_map/all_to_all | solution.py:123
  74.2 9.9 %all-to-all-start.1 = ((bf16[1,8,32,256]{3,1,0,2:T(8,128)(2,1)}), bf16[1,8,32,256]{3,1,0,2:T(8,128)(2,1)}, u32[]{:S(2)}, u32[]{:S(2)}) async-start(bf16[1,8,32,256]{3,1,0,2:T(8,128)(2,1)} %reshape.619), calls=%async_computation.1 | async-start | bytes 262144 | tf_op jit(solution)/shard_map/all_to_all | solution.py:131
  84.1 14.1 %all-to-all-start.3 = ((bf16[1,8,32,768]{3,1,0,2:T(8,128)(2,1)}), bf16[1,8,32,768]{3,1,0,2:T(8,128)(2,1)}, u32[]{:S(2)}, u32[]{:S(2)}) async-start(bf16[1,8,32,768]{3,1,0,2:T(8,128)(2,1)} %copy.93), calls=%async_computation.3 | async-start | bytes 786432 | tf_op jit(solution)/shard_map/all_to_all | solution.py:148
  89.3 75.1 %all-reduce.5.cloned.1.call-start = ((), (), s32[]{:S(2)}) async-start(), calls=%async_computation.4 | async-start | bytes 4423680 | tf_op jit(solution)/shard_map/psum | solution.py:171
  112.6 144.9 %all-reduce.7.cloned.1.call-start = ((), (), s32[]{:S(2)}) async-start(), calls=%async_computation.5 | async-start | bytes 4423680 | tf_op jit(solution)/shard_map/psum | solution.py:172
  164.5 8.2 %collective-permute-start.4 = (bf16[1,32,3,512]{3,2,1,0:T(4,128)(2,1)S(1)}, bf16[1,32,3,512]{3,2,1,0:T(4,128)(2,1)S(1)}, u32[]{:S(2)}, u32[]{:S(2)}) collective-permute-start(bf16[1,32,3,512]{3,2,1,0:T(4,128)(2,1)S(1)} %get-tuple-element.94), channel_id=1, source_target_pairs={{0,4},{4,8},{8,12},{12,0},{1,5},{5,9},{9,13},{13,1},{2,6},{6,10},{... | collective-permute-start | bytes 294920 | tf_op jit(solution)/shard_map/ppermute | solution.py:18
  166.1 7.6 %collective-permute-start.5 = (bf16[1,32,3,512]{3,2,1,0:T(4,128)(2,1)S(1)}, bf16[1,32,3,512]{3,2,1,0:T(4,128)(2,1)S(1)}, u32[]{:S(2)}, u32[]{:S(2)}) collective-permute-start(bf16[1,32,3,512]{3,2,1,0:T(4,128)(2,1)S(1)} %get-tuple-element.95), channel_id=1, source_target_pairs={{4,0},{8,4},{12,8},{0,12},{5,1},{9,5},{13,9},{1,13},{6,2},{10,6},{... | collective-permute-start | bytes 294920 | tf_op jit(solution)/shard_map/ppermute | solution.py:19
  173.7 24.0 %collective-permute-start.6 = (bf16[1,3,14,512]{3,2,1,0:T(8,128)(2,1)S(1)}, bf16[1,3,14,512]{3,2,1,0:T(8,128)(2,1)S(1)}, u32[]{:S(2)}, u32[]{:S(2)}) collective-permute-start(bf16[1,3,14,512]{3,2,1,0:T(8,128)(2,1)S(1)} %get-tuple-element.83), channel_id=1, source_target_pairs={{0,2},{1,3},{4,6},{5,7},{8,10},{9,11},{12,14},{13,15},{16,18},{17,... | collective-permute-start | bytes 129032 | tf_op jit(solution)/shard_map/ppermute | solution.py:18
  176.3 21.5 %collective-permute-start.7 = (bf16[1,3,14,512]{3,2,1,0:T(8,128)(2,1)S(1)}, bf16[1,3,14,512]{3,2,1,0:T(8,128)(2,1)S(1)}, u32[]{:S(2)}, u32[]{:S(2)}) collective-permute-start(bf16[1,3,14,512]{3,2,1,0:T(8,128)(2,1)S(1)} %get-tuple-element.84), channel_id=1, source_target_pairs={{2,0},{3,1},{6,4},{7,5},{10,8},{11,9},{14,12},{15,13},{18,16},{19,... | collective-permute-start | bytes 129032 | tf_op jit(solution)/shard_map/ppermute | solution.py:19
  177.6 20.4 %copy-start.20 = (f32[1,1,512]{2,1,0:T(1,128)S(1)}, f32[1,1,512]{2,1,0:T(1,128)}, u32[]{:S(2)}) copy-start(f32[1,1,512]{2,1,0:T(1,128)} %copy-done.19) | copy-start | bytes 6148
  177.6 20.4 %copy-start.22 = (f32[1,1,512]{2,1,0:T(1,128)S(1)}, f32[1,1,512]{2,1,0:T(1,128)}, u32[]{:S(2)}) copy-start(f32[1,1,512]{2,1,0:T(1,128)} %copy-done.21) | copy-start | bytes 6148
  177.6 20.4 %copy-start.24 = (f32[1,1,512]{2,1,0:T(1,128)S(1)}, f32[1,1,512]{2,1,0:T(1,128)}, u32[]{:S(2)}) copy-start(f32[1,1,512]{2,1,0:T(1,128)} %copy-done.23) | copy-start | bytes 6148
  177.6 20.4 %copy-start.26 = (f32[1,1,512]{2,1,0:T(1,128)S(1)}, f32[1,1,512]{2,1,0:T(1,128)}, u32[]{:S(2)}) copy-start(f32[1,1,512]{2,1,0:T(1,128)} %copy-done.25) | copy-start | bytes 6148
  177.6 20.4 %copy-start.28 = (f32[1,1,512]{2,1,0:T(1,128)S(1)}, f32[1,1,512]{2,1,0:T(1,128)}, u32[]{:S(2)}) copy-start(f32[1,1,512]{2,1,0:T(1,128)} %copy-done.27) | copy-start | bytes 6148
  177.6 20.4 %copy-start.30 = (f32[1,1,512]{2,1,0:T(1,128)S(1)}, f32[1,1,512]{2,1,0:T(1,128)}, u32[]{:S(2)}) copy-start(f32[1,1,512]{2,1,0:T(1,128)} %copy-done.29) | copy-start | bytes 6148
  177.6 20.4 %copy-start.32 = (f32[1,1,512]{2,1,0:T(1,128)S(1)}, f32[1,1,512]{2,1,0:T(1,128)}, u32[]{:S(2)}) copy-start(f32[1,1,512]{2,1,0:T(1,128)} %copy-done.31) | copy-start | bytes 6148
  177.6 20.4 %copy-start.34 = (f32[1,1,512]{2,1,0:T(1,128)S(1)}, f32[1,1,512]{2,1,0:T(1,128)}, u32[]{:S(2)}) copy-start(f32[1,1,512]{2,1,0:T(1,128)} %copy-done.33) | copy-start | bytes 6148
  177.7 20.4 %copy-start.36 = (f32[1,1,512]{2,1,0:T(1,128)S(1)}, f32[1,1,512]{2,1,0:T(1,128)}, u32[]{:S(2)}) copy-start(f32[1,1,512]{2,1,0:T(1,128)} %copy-done.35) | copy-start | bytes 6148
  177.7 20.4 %copy-start.38 = (f32[1,1,512]{2,1,0:T(1,128)S(1)}, f32[1,1,512]{2,1,0:T(1,128)}, u32[]{:S(2)}) copy-start(f32[1,1,512]{2,1,0:T(1,128)} %copy-done.37) | copy-start | bytes 6148
  177.7 20.4 %copy-start.39 = (f32[1,1,512]{2,1,0:T(1,128)S(1)}, f32[1,1,512]{2,1,0:T(1,128)}, u32[]{:S(2)}) copy-start(f32[1,1,512]{2,1,0:T(1,128)} %get-tuple-element.111) | copy-start | bytes 6148
  177.7 20.4 %copy-start.40 = (f32[1,1,512]{2,1,0:T(1,128)S(1)}, f32[1,1,512]{2,1,0:T(1,128)}, u32[]{:S(2)}) copy-start(f32[1,1,512]{2,1,0:T(1,128)} %get-tuple-element.112) | copy-start | bytes 6148
  177.7 20.4 %copy-start.41 = (f32[1,1,512]{2,1,0:T(1,128)S(1)}, f32[1,1,512]{2,1,0:T(1,128)}, u32[]{:S(2)}) copy-start(f32[1,1,512]{2,1,0:T(1,128)} %get-tuple-element.113) | copy-start | bytes 6148
  177.7 20.4 %copy-start.42 = (f32[1,1,512]{2,1,0:T(1,128)S(1)}, f32[1,1,512]{2,1,0:T(1,128)}, u32[]{:S(2)}) copy-start(f32[1,1,512]{2,1,0:T(1,128)} %get-tuple-element.114) | copy-start | bytes 6148
  177.7 20.4 %copy-start.43 = (f32[1,1,512]{2,1,0:T(1,128)S(1)}, f32[1,1,512]{2,1,0:T(1,128)}, u32[]{:S(2)}) copy-start(f32[1,1,512]{2,1,0:T(1,128)} %get-tuple-element.115) | copy-start | bytes 6148
  177.7 20.4 %copy-start.44 = (f32[1,1,512]{2,1,0:T(1,128)S(1)}, f32[1,1,512]{2,1,0:T(1,128)}, u32[]{:S(2)}) copy-start(f32[1,1,512]{2,1,0:T(1,128)} %get-tuple-element.116) | copy-start | bytes 6148
  177.7 20.4 %copy-start.45 = (f32[1,1,512]{2,1,0:T(1,128)S(1)}, f32[1,1,512]{2,1,0:T(1,128)}, u32[]{:S(2)}) copy-start(f32[1,1,512]{2,1,0:T(1,128)} %get-tuple-element.117) | copy-start | bytes 6148
  177.7 20.4 %copy-start.46 = (f32[1,1,512]{2,1,0:T(1,128)S(1)}, f32[1,1,512]{2,1,0:T(1,128)}, u32[]{:S(2)}) copy-start(f32[1,1,512]{2,1,0:T(1,128)} %get-tuple-element.118) | copy-start | bytes 6148
  177.8 20.4 %copy-start.47 = (f32[1,1,512]{2,1,0:T(1,128)S(1)}, f32[1,1,512]{2,1,0:T(1,128)}, u32[]{:S(2)}) copy-start(f32[1,1,512]{2,1,0:T(1,128)} %get-tuple-element.119) | copy-start | bytes 6148
  177.8 20.4 %copy-start.48 = (f32[1,1,512]{2,1,0:T(1,128)S(1)}, f32[1,1,512]{2,1,0:T(1,128)}, u32[]{:S(2)}) copy-start(f32[1,1,512]{2,1,0:T(1,128)} %get-tuple-element.120) | copy-start | bytes 6148
  177.8 20.4 %copy-start.49 = (f32[1,1,512]{2,1,0:T(1,128)S(1)}, f32[1,1,512]{2,1,0:T(1,128)}, u32[]{:S(2)}) copy-start(f32[1,1,512]{2,1,0:T(1,128)} %get-tuple-element.121) | copy-start | bytes 6148
  177.8 20.4 %copy-start.50 = (f32[1,1,512]{2,1,0:T(1,128)S(1)}, f32[1,1,512]{2,1,0:T(1,128)}, u32[]{:S(2)}) copy-start(f32[1,1,512]{2,1,0:T(1,128)} %get-tuple-element.122) | copy-start | bytes 6148
  177.8 20.4 %copy-start.51 = (f32[1,1,512]{2,1,0:T(1,128)S(1)}, f32[1,1,512]{2,1,0:T(1,128)}, u32[]{:S(2)}) copy-start(f32[1,1,512]{2,1,0:T(1,128)} %get-tuple-element.123) | copy-start | bytes 6148
  177.8 20.4 %copy-start.52 = (f32[1,1,512]{2,1,0:T(1,128)S(1)}, f32[1,1,512]{2,1,0:T(1,128)}, u32[]{:S(2)}) copy-start(f32[1,1,512]{2,1,0:T(1,128)} %get-tuple-element.124) | copy-start | bytes 6148
  177.8 20.4 %copy-start.53 = (f32[1,1,512]{2,1,0:T(1,128)S(1)}, f32[1,1,512]{2,1,0:T(1,128)}, u32[]{:S(2)}) copy-start(f32[1,1,512]{2,1,0:T(1,128)} %get-tuple-element.125) | copy-start | bytes 6148
  177.8 20.4 %copy-start.54 = (f32[1,1,512]{2,1,0:T(1,128)S(1)}, f32[1,1,512]{2,1,0:T(1,128)}, u32[]{:S(2)}) copy-start(f32[1,1,512]{2,1,0:T(1,128)} %get-tuple-element.126) | copy-start | bytes 6148
  177.8 20.4 %copy-start.55 = (f32[1,1,512]{2,1,0:T(1,128)S(1)}, f32[1,1,512]{2,1,0:T(1,128)}, u32[]{:S(2)}) copy-start(f32[1,1,512]{2,1,0:T(1,128)} %get-tuple-element.127) | copy-start | bytes 6148
  177.8 20.4 %copy-start.56 = (f32[1,1,512]{2,1,0:T(1,128)S(1)}, f32[1,1,512]{2,1,0:T(1,128)}, u32[]{:S(2)}) copy-start(f32[1,1,512]{2,1,0:T(1,128)} %get-tuple-element.128) | copy-start | bytes 6148
  177.9 20.4 %copy-start.57 = (f32[1,1,512]{2,1,0:T(1,128)S(1)}, f32[1,1,512]{2,1,0:T(1,128)}, u32[]{:S(2)}) copy-start(f32[1,1,512]{2,1,0:T(1,128)} %get-tuple-element.129) | copy-start | bytes 6148
  177.9 20.4 %copy-start.58 = (f32[1,1,512]{2,1,0:T(1,128)S(1)}, f32[1,1,512]{2,1,0:T(1,128)}, u32[]{:S(2)}) copy-start(f32[1,1,512]{2,1,0:T(1,128)} %get-tuple-element.130) | copy-start | bytes 6148
  177.9 20.4 %copy-start.59 = (f32[1,1,512]{2,1,0:T(1,128)S(1)}, f32[1,1,512]{2,1,0:T(1,128)}, u32[]{:S(2)}) copy-start(f32[1,1,512]{2,1,0:T(1,128)} %get-tuple-element.131) | copy-start | bytes 6148
  177.9 20.4 %copy-start.60 = (f32[1,1,512]{2,1,0:T(1,128)S(1)}, f32[1,1,512]{2,1,0:T(1,128)}, u32[]{:S(2)}) copy-start(f32[1,1,512]{2,1,0:T(1,128)} %get-tuple-element.132) | copy-start | bytes 6148
  177.9 20.4 %copy-start.61 = (f32[1,1,512]{2,1,0:T(1,128)S(1)}, f32[1,1,512]{2,1,0:T(1,128)}, u32[]{:S(2)}) copy-start(f32[1,1,512]{2,1,0:T(1,128)} %get-tuple-element.133) | copy-start | bytes 6148
  177.9 20.4 %copy-start.62 = (f32[1,1,512]{2,1,0:T(1,128)S(1)}, f32[1,1,512]{2,1,0:T(1,128)}, u32[]{:S(2)}) copy-start(f32[1,1,512]{2,1,0:T(1,128)} %get-tuple-element.134) | copy-start | bytes 6148
  177.9 20.4 %copy-start.63 = (f32[1,1,512]{2,1,0:T(1,128)S(1)}, f32[1,1,512]{2,1,0:T(1,128)}, u32[]{:S(2)}) copy-start(f32[1,1,512]{2,1,0:T(1,128)} %get-tuple-element.135) | copy-start | bytes 6148
  177.9 20.4 %copy-start.64 = (f32[1,1,512]{2,1,0:T(1,128)S(1)}, f32[1,1,512]{2,1,0:T(1,128)}, u32[]{:S(2)}) copy-start(f32[1,1,512]{2,1,0:T(1,128)} %get-tuple-element.136) | copy-start | bytes 6148
  177.9 20.4 %copy-start.65 = (f32[1,1,512]{2,1,0:T(1,128)S(1)}, f32[1,1,512]{2,1,0:T(1,128)}, u32[]{:S(2)}) copy-start(f32[1,1,512]{2,1,0:T(1,128)} %get-tuple-element.137) | copy-start | bytes 6148
  177.9 20.4 %copy-start.66 = (f32[1,1,512]{2,1,0:T(1,128)S(1)}, f32[1,1,512]{2,1,0:T(1,128)}, u32[]{:S(2)}) copy-start(f32[1,1,512]{2,1,0:T(1,128)} %get-tuple-element.138) | copy-start | bytes 6148
  178.9 19.5 %copy-start.67 = (f32[1,1,512]{2,1,0:T(1,128)S(1)}, f32[1,1,512]{2,1,0:T(1,128)}, u32[]{:S(2)}) copy-start(f32[1,1,512]{2,1,0:T(1,128)} %get-tuple-element.139) | copy-start | bytes 6148
  178.9 19.5 %copy-start.68 = (f32[1,1,512]{2,1,0:T(1,128)S(1)}, f32[1,1,512]{2,1,0:T(1,128)}, u32[]{:S(2)}) copy-start(f32[1,1,512]{2,1,0:T(1,128)} %get-tuple-element.140) | copy-start | bytes 6148
  (31 other events, 167.3 us)
Sparse Core Ops, SparseCore 0:
  112.7 51.6 all-reduce.4
  167.0 90.4 all-reduce.6
